TPU v7x, 32 devices: a whole 2x2x4 slice. The times are simulated.
32 devices in a mesh: seq: 8 (over z, y), grp: 4 (over x, core).
Axes of the slice: x: 2, y: 2, z: 4, core: 2. Of those that a mesh axis runs over, the one named last changes fastest.
Arguments:
- queries: bfloat16 [2048, 5120], P('seq', 'grp'), may hold values from -64 to 64
- keys: bfloat16 [2048, 5120], P('seq', 'grp'), may hold values from -4 to 4
- values: bfloat16 [2048, 5120], P('seq', 'grp'), may hold values from -24 to 24
- cluster_of: int32 [2048], P('seq'), may hold values from 0 to 15, as said below
- pair_mask: int32 [16, 16], replicated, may hold values from 0 to 1, as said below
- out_weight: bfloat16 [5120, 5120], P('grp'), may hold values from -0.078125 to 0.078125
Outputs:
- mixed: bfloat16 [2048, 5120], P('seq', 'grp')
Inputs may be any that keep to these rules, and one draw needn't show every extreme that they name: `cluster_of`: of the 256 tokens at one index of seq, at most 64 have a cluster c with c // 2 equal to any one j, and in every draw some index sends exactly 64 to some j. A cluster holds at most 256 tokens, and in every draw some cluster holds exactly 256. pair_mask[c, c] = 1 for every cluster c.
All inputs are finite; a program needn't handle non-finite values.
Results may differ from a plain program's by a relative error of at most 0.013.
Values may be sent and summed in bfloat16 or wider, within the bound.
A program may use at most 128 MiB of HBM per device.

v0:
```python
import jax
import jax.numpy as jnp
from jax import lax
from jax.sharding import PartitionSpec as P

HD = 128


NEG = -1e30


def prefix(shard, axis, combine, identity):
    count, place = (lax.axis_size(axis), lax.axis_index(axis))
    everything = lax.all_gather(shard, axis)
    start = jnp.broadcast_to(jnp.asarray(identity, shard.dtype), shard.shape)

    def lap(k, before):
        reached = k < place
        new = combine(before, everything[k])
        return jnp.where(reached, new, before)

    return lax.fori_loop(0, count, lap, start)


def add_counts(earlier, later):
    return earlier + later


def start_state(row_count, heads):
    return (
        jnp.full((row_count, heads), NEG, jnp.float32),
        jnp.zeros((row_count, heads), jnp.float32),
        jnp.zeros((row_count, heads, HD), jnp.float32),
    )


def attend(carried, query_rows, key_block, value_block, allowed):
    best_score, row_total, weighted = carried
    row_count = query_rows.shape[0]
    heads = best_score.shape[1]
    query_heads = query_rows.reshape(row_count, heads, HD)
    key_heads = key_block.reshape(key_block.shape[0], heads, HD)
    value_heads = value_block.reshape(value_block.shape[0], heads, HD)
    scores = jnp.einsum(
        "qhd,khd->qhk", query_heads, key_heads, preferred_element_type=jnp.float32
    ) * HD ** (-0.5)
    keep_mask = allowed[:, None, :]
    scores = jnp.where(keep_mask, scores, NEG)
    new_best = jnp.maximum(best_score, jnp.max(scores, axis=2))
    factor = jnp.exp(best_score - new_best)
    weights = jnp.where(keep_mask, jnp.exp(scores - new_best[:, :, None]), 0.0)
    row_total = row_total * factor + jnp.sum(weights, axis=2)
    weighted = weighted * factor[:, :, None] + jnp.einsum(
        "qhk,khd->qhd",
        weights.astype(jnp.bfloat16),
        value_heads,
        preferred_element_type=jnp.float32,
    )
    return (new_best, row_total, weighted)


def fold_blocks(carried, query_rows, key_piece, value_piece, allowed_of, span_rows):
    row_count = key_piece.shape[0]

    def one_block(block_index, running):
        first_row = block_index * span_rows
        key_block = lax.dynamic_slice_in_dim(key_piece, first_row, span_rows, 0)
        value_block = lax.dynamic_slice_in_dim(value_piece, first_row, span_rows, 0)
        allowed = allowed_of(first_row, span_rows)
        return attend(running, query_rows, key_block, value_block, allowed)

    return lax.fori_loop(0, row_count // span_rows, one_block, carried)


def finish_rows(carried):
    best_score, row_total, weighted = carried
    safe_total = jnp.where(row_total > 0.0, row_total, 1.0)
    result = jnp.where(row_total[:, :, None] > 0.0, weighted / safe_total[:, :, None], 0.0)
    return result.reshape(result.shape[0], -1).astype(jnp.bfloat16)


def body(queries, keys, values, cluster_of, pair_mask, out_weight):
    seq_count = lax.axis_size("seq")
    seq_index = lax.axis_index("seq")
    tok_rows, width_here = queries.shape
    heads = width_here // HD
    clusters = pair_mask.shape[0]
    per_owner = clusters // seq_count
    capacity = 2 * tok_rows // per_owner
    pair_rows = 2 * tok_rows // seq_count
    mask_float = pair_mask.astype(jnp.float32)
    cluster_ids = jnp.arange(clusters, dtype=jnp.int32)

    def key_hot(key_cluster):
        return (key_cluster[:, None] == cluster_ids[None, :]).astype(jnp.float32)

    onehot = (cluster_of[:, None] == cluster_ids[None, :]).astype(jnp.int32)
    counts = jnp.sum(onehot, axis=0)
    earlier_here = jnp.cumsum(onehot, axis=0) - onehot
    offsets = prefix(counts, "seq", add_counts, jnp.zeros_like(counts))
    slot_index = jnp.sum((earlier_here + offsets[None, :]) * onehot, axis=1)
    owner = cluster_of // per_owner
    panel_row = cluster_of % per_owner * capacity + slot_index
    owner_hot = (owner[:, None] == jnp.arange(seq_count, dtype=jnp.int32)[None, :]).astype(
        jnp.int32
    )
    bucket_place = jnp.sum((jnp.cumsum(owner_hot, axis=0) - owner_hot) * owner_hot, axis=1)
    send_row = owner * pair_rows + bucket_place
    slots_all = seq_count * pair_rows
    panel_size = per_owner * capacity

    def pack_rows(rows_in):
        return jnp.zeros((slots_all, rows_in.shape[1]), rows_in.dtype).at[send_row].set(rows_in)

    meta_rows = jnp.full((slots_all,), panel_size, jnp.int32).at[send_row].set(panel_row)
    got_queries, got_keys, got_values, got_meta = (
        lax.all_to_all(pack_rows(queries), "seq", split_axis=0, concat_axis=0, tiled=True),
        lax.all_to_all(pack_rows(keys), "seq", split_axis=0, concat_axis=0, tiled=True),
        lax.all_to_all(pack_rows(values), "seq", split_axis=0, concat_axis=0, tiled=True),
        lax.all_to_all(meta_rows, "seq", split_axis=0, concat_axis=0, tiled=True),
    )

    def unpack_rows(rows_in):
        return (
            jnp.zeros((panel_size, rows_in.shape[1]), rows_in.dtype)
            .at[got_meta]
            .set(rows_in, mode="drop")
        )

    query_panel = unpack_rows(got_queries)
    key_panel = unpack_rows(got_keys)
    value_panel = unpack_rows(got_values)
    filled = jnp.zeros((panel_size,), jnp.int32).at[got_meta].set(1, mode="drop")
    query_cluster = seq_index * per_owner + jnp.arange(panel_size, dtype=jnp.int32) // capacity
    rows_mask = jnp.dot(key_hot(query_cluster), mask_float)
    carried = start_state(panel_size, heads)
    key_piece = lax.all_gather(key_panel, "seq", axis=0, tiled=True)
    value_piece = lax.all_gather(value_panel, "seq", axis=0, tiled=True)
    filled_piece = lax.all_gather(filled, "seq", axis=0, tiled=True)
    results = []
    for query_group in range(per_owner):
        low = query_group * capacity
        group_mask = rows_mask[low : low + capacity]
        group_state = tuple((item[low : low + capacity] for item in carried))

        def allowed_of(first_row, span_rows, group_mask=group_mask):
            key_cluster = (first_row + jnp.arange(span_rows, dtype=jnp.int32)) // capacity
            paired = jnp.dot(group_mask, key_hot(key_cluster).T) > 0.5
            live_rows = lax.dynamic_slice_in_dim(filled_piece, first_row, span_rows, 0) > 0
            return paired & live_rows[None, :]

        results.append(
            fold_blocks(
                group_state,
                query_panel[low : low + capacity],
                key_piece,
                value_piece,
                allowed_of,
                capacity,
            )
        )
    state_out = tuple(
        (jnp.concatenate([result[member] for result in results], axis=0) for member in range(3))
    )
    attn_panel = finish_rows(state_out)
    picked = jnp.where(
        (got_meta < panel_size)[:, None],
        attn_panel[jnp.minimum(got_meta, panel_size - 1)],
        jnp.zeros((), jnp.bfloat16),
    )
    returned = lax.all_to_all(picked, "seq", split_axis=0, concat_axis=0, tiled=True)
    attn_tok = returned[send_row]
    terms = jnp.dot(attn_tok, out_weight, preferred_element_type=jnp.float32)
    mixed = lax.psum_scatter(terms.astype(jnp.bfloat16), "grp", scatter_dimension=1, tiled=True)
    return mixed


def solution(mesh):
    in_specs = (P("seq", "grp"), P("seq", "grp"), P("seq", "grp"), P("seq"), P(), P("grp", None))
    out_specs = P("seq", "grp")
    return jax.shard_map(body, mesh=mesh, in_specs=in_specs, out_specs=out_specs, check_vma=False)
```

profile of v0, /device:TPU:0, one launch (start us, length us, event | category | flops | bytes accessed | tf_op | source)
XLA Modules:
  0.0 768.8 jit_solution(2374137955772319222)
XLA Ops:
  9.6 13.1 %all-reduce = s32[128]{0:T(128)S(1)} all-reduce(s32[128]{0:T(128)S(1)} %dynamic-update-slice), channel_id=2, replica_groups=mesh['seq'=8,'grp'=4] {'seq'}, use_global_device_ids=true, to_apply=%add | all-reduce | flops 128 | bytes 1024
  29.0 3.3 all-to-all-start
  32.4 3.5 scatter_custom_fusion.2
  35.8 2.9 all-to-all-done
  38.7 3.6 all-to-all-start.1
  43.6 26.6 %all-to-all-done.1 = bf16[8,64,1280]{2,1,0:T(8,128)(2,1)S(1)} async-done(((bf16[8,64,1280]{2,1,0:T(8,128)(2,1)}), bf16[8,64,1280]{2,1,0:T(8,128)(2,1)S(1)}, u32[]{:S(2)}, u32[]{:S(2)}) %all-to-all-start.1) | async-done | bytes 1310752 | tf_op jit(solution)/shard_map/all_to_all | solution.py:118
  70.2 3.9 scatter_custom_fusion.3
  74.2 2.7 scatter_custom_fusion.6
  76.9 66.0 %all_to_all.57 = bf16[8,64,1280]{2,1,0:T(8,128)(2,1)S(1)} all-to-all(bf16[8,64,1280]{2,1,0:T(8,128)(2,1)S(1)} %bitcast.152), channel_id=1, replica_groups=mesh['seq'=8,'grp'=4] {'seq'}, dimensions={0} | all-to-all | bytes 2621440 | tf_op jit(solution)/shard_map/all_to_all | solution.py:119
  142.8 3.9 scatter_custom_fusion.7
  146.8 3.5 scatter_custom_fusion.4
  150.3 4.2 all-to-all-start.2
  154.8 2.4 scatter_custom_fusion.1
  157.2 82.5 %all-gather.1 = s32[8,1,512]{2,1,0:T(1,128)S(1)} all-gather(s32[1,1,512]{2,1,0:T(1,128)S(1)} %bitcast.164), channel_id=1, replica_groups=mesh['seq'=8,'grp'=4] {'seq'}, dimensions={0}, use_global_device_ids=true | all-gather | bytes 18432 | tf_op jit(solution)/shard_map/all_gather | solution.py:139
  239.8 3.4 scatter_custom_fusion.5
  244.5 23.0 %all-gather.5.cloned.1.call-done = bf16[4096,1280]{1,0:T(8,128)(2,1)} async-done(((bf16[512,1280]{1,0:T(8,128)(2,1)}), bf16[4096,1280]{1,0:T(8,128)(2,1)}) %all-gather.5.cloned.1.call-update) | async-done | bytes 10485776 | tf_op jit(solution)/shard_map/all_gather | solution.py:137
  267.6 14.4 %copy.64 = bf16[4096,1280]{0,1:T(8,128)(2,1)} copy(bf16[4096,1280]{1,0:T(8,128)(2,1)} %all-gather.5.cloned.1.call-done) | data formatting | bytes 20971520
  282.0 137.3 %all-gather.7.cloned.1.call-done = bf16[4096,1280]{1,0:T(8,128)(2,1)} async-done(((bf16[512,1280]{1,0:T(8,128)(2,1)}), bf16[4096,1280]{1,0:T(8,128)(2,1)}) %all-gather.7.cloned.1.call-update) | async-done | bytes 10485776 | tf_op jit(solution)/shard_map/all_gather | solution.py:138
  419.3 14.3 %copy.66 = bf16[4096,1280]{0,1:T(8,128)(2,1)} copy(bf16[4096,1280]{1,0:T(8,128)(2,1)} %all-gather.7.cloned.1.call-done) | data formatting | bytes 20971520
  433.6 127.1 %while.56 = (s32[]{:T(128)}, f32[256,10]{0,1:T(8,128)S(1)}, f32[256,10]{0,1:T(8,128)S(1)}, f32[256,10,128]{0,2,1:T(8,128)}, bf16[256,16]{0,1:T(8,128)(2,1)S(1)},...) while((s32[]{:T(128)}, f32[256,10]{0,1:T(8,128)S(1)}, ...), condition=%wide.region_24.25_spmd.clone, body=%wide.region_21.24_spmd.clone.sunk | while | flops 347296512 | bytes 28618516 | solution.py:72
  433.9 2.2 constant_dynamic-slice_fusion.7
  436.2 1.7 fusion.120
  441.9 2.2 constant_dynamic-slice_fusion.7
  449.8 2.2 constant_dynamic-slice_fusion.7
  457.8 2.2 constant_dynamic-slice_fusion.7
  465.7 2.2 constant_dynamic-slice_fusion.7
  473.6 2.2 constant_dynamic-slice_fusion.7
  481.6 2.2 constant_dynamic-slice_fusion.7
  489.5 2.2 constant_dynamic-slice_fusion.7
  497.5 2.2 constant_dynamic-slice_fusion.7
  499.7 1.7 fusion.120
  505.4 2.2 constant_dynamic-slice_fusion.7
  507.6 1.7 fusion.120
  513.4 2.2 constant_dynamic-slice_fusion.7
  521.3 2.2 constant_dynamic-slice_fusion.7
  529.2 2.2 constant_dynamic-slice_fusion.7
  537.2 2.2 constant_dynamic-slice_fusion.7
  545.1 2.2 constant_dynamic-slice_fusion.7
  553.1 2.2 constant_dynamic-slice_fusion.7
  560.7 109.7 %while.55 = (s32[]{:T(128)}, f32[256,10]{0,1:T(8,128)S(1)}, f32[256,10]{0,1:T(8,128)S(1)}, f32[256,10,128]{0,2,1:T(8,128)}, bf16[256,16]{0,1:T(8,128)(2,1)S(1)},...) while((s32[]{:T(128)}, f32[256,10]{0,1:T(8,128)S(1)}, ...), condition=%wide.region_20.21_spmd.clone, body=%wide.region_17.20_spmd.clone.sunk | while | flops 347296512 | bytes 28618516 | solution.py:72
  561.0 2.2 constant_dynamic-slice_fusion.6
  567.9 2.2 constant_dynamic-slice_fusion.6
  574.7 2.2 constant_dynamic-slice_fusion.6
  581.6 2.2 constant_dynamic-slice_fusion.6
  588.4 2.2 constant_dynamic-slice_fusion.6
  595.3 2.2 constant_dynamic-slice_fusion.6
  602.1 2.2 constant_dynamic-slice_fusion.6
  609.0 2.2 constant_dynamic-slice_fusion.6
  615.8 2.2 constant_dynamic-slice_fusion.6
  622.7 2.2 constant_dynamic-slice_fusion.6
  629.6 2.2 constant_dynamic-slice_fusion.6
  636.4 2.2 constant_dynamic-slice_fusion.6
  643.3 2.2 constant_dynamic-slice_fusion.6
  650.1 2.2 constant_dynamic-slice_fusion.6
  657.0 2.2 constant_dynamic-slice_fusion.6
  663.8 2.2 constant_dynamic-slice_fusion.6
  670.7 2.1 copy.72
  674.1 1.8 copy.71
  677.5 2.7 fusion.39
  680.1 2.1 gather_fusion
  683.5 3.6 all-to-all-start.4
  687.4 30.5 %all-to-all-done.4 = bf16[8,64,1280]{2,1,0:T(8,128)(2,1)S(1)} async-done(((bf16[8,64,1280]{2,1,0:T(8,128)(2,1)}), bf16[8,64,1280]{2,1,0:T(8,128)(2,1)S(1)}, u32[]{:S(2)}, u32[]{:S(2)}) %all-to-all-start.4) | async-done | bytes 1310752 | tf_op jit(solution)/shard_map/all_to_all | solution.py:171
  719.2 9.6 %convolution_convert_fusion = bf16[256,5120]{1,0:T(8,128)(2,1)} fusion(bf16[256,1280]{1,0:T(8,128)(2,1)S(1)} %gather_fusion.1, bf16[1280,5120]{1,0:T(8,128)(2,1)} %param.17), kind=kOutput, calls=%fused_computation.78 | convolution fusion | flops 3356753920 | bytes 16384000 | tf_op jit(solution)/shard_map/dot_general | solution.py:173
  728.8 33.5 %reduce-scatter.2.cloned.1.call-done = bf16[256,1280]{1,0:T(8,128)(2,1)} async-done(((bf16[256,5120]{1,0:T(8,128)(2,1)}), bf16[256,1280]{1,0:T(8,128)(2,1)}) %reduce-scatter.2.cloned.1.call-update) | async-done | bytes 655376 | tf_op jit(solution)/shard_map/reduce_scatter | solution.py:174
  (549 shorter events, 175.7 us)
Async XLA Ops:
  29.0 9.7 %all-to-all-start = ((s32[8,64,1]{1,2,0:T(1,128)}), s32[8,64,1]{1,2,0:T(1,128)S(1)}, u32[]{:S(2)}, u32[]{:S(2)}) async-start(s32[8,64,1]{1,2,0:T(1,128)} %all_to_all.38), calls=%async_computation | async-start | bytes 8192 | tf_op jit(solution)/shard_map/all_to_all | solution.py:120
  38.7 31.5 %all-to-all-start.1 = ((bf16[8,64,1280]{2,1,0:T(8,128)(2,1)}), bf16[8,64,1280]{2,1,0:T(8,128)(2,1)S(1)}, u32[]{:S(2)}, u32[]{:S(2)}) async-start(bf16[8,64,1280]{2,1,0:T(8,128)(2,1)} %bitcast.11), calls=%async_computation.1 | async-start | bytes 2621440 | tf_op jit(solution)/shard_map/all_to_all | solution.py:118
  42.3 225.3 %all-gather.5.cloned.1.call-start = ((), (), s32[]{:S(2)}) async-start(), calls=%async_computation.6 | async-start | bytes 11796480 | tf_op jit(solution)/shard_map/all_gather | solution.py:137
  74.1 345.2 %all-gather.7.cloned.1.call-start = ((), (), s32[]{:S(2)}) async-start(), calls=%async_computation.7 | async-start | bytes 11796480 | tf_op jit(solution)/shard_map/all_gather | solution.py:138
  150.3 4.2 copy-start.7
  150.3 89.5 %all-to-all-start.2 = ((bf16[8,64,1280]{2,1,0:T(8,128)(2,1)}), bf16[8,64,1280]{2,1,0:T(8,128)(2,1)S(1)}, u32[]{:S(2)}, u32[]{:S(2)}) async-start(bf16[8,64,1280]{2,1,0:T(8,128)(2,1)} %bitcast.13), calls=%async_computation.2 | async-start | bytes 2621440 | tf_op jit(solution)/shard_map/all_to_all | solution.py:117
  437.9 1.1 copy-start
  437.9 1.5 copy-start.5
  445.8 1.1 copy-start
  445.8 1.5 copy-start.5
  453.8 1.1 copy-start
  453.8 1.5 copy-start.5
  461.7 1.1 copy-start
  461.7 1.5 copy-start.5
  469.7 1.1 copy-start
  469.7 1.5 copy-start.5
  477.6 1.5 copy-start.5
  485.6 1.5 copy-start.5
  493.5 1.1 copy-start
  493.5 1.5 copy-start.5
  501.4 1.5 copy-start.5
  509.4 1.5 copy-start.5
  517.3 1.5 copy-start.5
  525.3 1.5 copy-start.5
  533.2 1.5 copy-start.5
  541.2 1.5 copy-start.5
  549.1 1.1 copy-start
  549.1 1.5 copy-start.5
  557.0 1.5 copy-start.5
  563.9 1.1 copy-start.1
  563.9 1.5 copy-start.2
  570.7 1.1 copy-start.1
  570.8 1.5 copy-start.2
  577.6 1.1 copy-start.1
  577.6 1.5 copy-start.2
  584.4 1.1 copy-start.1
  584.5 1.5 copy-start.2
  591.3 1.1 copy-start.1
  591.3 1.5 copy-start.2
  598.2 1.1 copy-start.1
  598.2 1.5 copy-start.2
  605.0 1.1 copy-start.1
  605.0 1.5 copy-start.2
  611.9 1.1 copy-start.1
  611.9 1.5 copy-start.2
  618.7 1.1 copy-start.1
  618.7 1.5 copy-start.2
  625.6 1.1 copy-start.1
  625.6 1.5 copy-start.2
  632.4 1.1 copy-start.1
  632.4 1.5 copy-start.2
  639.3 1.1 copy-start.1
  639.3 1.5 copy-start.2
  646.1 1.1 copy-start.1
  646.2 1.5 copy-start.2
  653.0 1.1 copy-start.1
  653.0 1.5 copy-start.2
  659.9 1.1 copy-start.1
  659.9 1.5 copy-start.2
  666.7 1.1 copy-start.1
  666.7 1.5 copy-start.2
  674.1 1.8 copy-start.4
  683.5 34.4 %all-to-all-start.4 = ((bf16[8,64,1280]{2,1,0:T(8,128)(2,1)}), bf16[8,64,1280]{2,1,0:T(8,128)(2,1)S(1)}, u32[]{:S(2)}, u32[]{:S(2)}) async-start(bf16[8,64,1280]{2,1,0:T(8,128)(2,1)} %broadcast_select_fusion.2), calls=%async_computation.4 | async-start | bytes 2621440 | tf_op jit(solution)/shard_map/all_to_all | solution.py:171
  687.1 75.2 %reduce-scatter.2.cloned.1.call-start = ((), (), s32[]{:S(2)}) async-start(), calls=%async_computation.8 | async-start | bytes 3276800 | tf_op jit(solution)/shard_map/reduce_scatter | solution.py:174
  (41 other events, 44.2 us)
Sparse Core Ops, SparseCore 0:
  74.3 193.2 all-gather.4
  269.8 149.5 all-gather.6
  728.9 33.3 reduce-scatter.1
where the time goes:
time: 773 us; the launch traced here: 769 us
  waiting for transfers between devices  254 us (33%)
  local copies, waits for them, and re-layouts  201 us (26%)
  blocking collectives  162 us (21%)
  matrix products  87.8 us (11%)
  other arithmetic  33 us (4%)
  starting transfers between devices  15 us (2%)
  between operations  14.1 us (2%)
    all_gather x1, waiting for transfers between devices, body(): value_piece = lax.all_gather(value_panel, 'seq', axis=0, tiled=True)  137 us
    all_gather x1, blocking collectives, body(): filled_piece = lax.all_gather(filled, 'seq', axis=0, tiled=True)  82.5 us
    dynamic_slice x32, local copies, waits for them, and re-layouts, one_block(): value_block = lax.dynamic_slice_in_dim(value_piece, first_row, span_rows, 0)  71.3 us
    all_to_all x1, blocking collectives, body(): lax.all_to_all(pack_rows(values), 'seq', split_axis=0, concat_axis=0, til...  66 us
    while x224, local copies, waits for them, and re-layouts  61.1 us
    dot_general x32, matrix products, attend(): jnp.einsum('qhd,khd->qhk', query_heads, key_heads, preferred_element_type...  37.3 us
    reduce_scatter x1, waiting for transfers between devices, body(): lax.psum_scatter(terms.astype(jnp.bfloat16), 'grp', scatter_dimension=1,...  33.5 us
    dot_general x32, matrix products, attend(): jnp.einsum('qhk,khd->qhd', weights.astype(jnp.bfloat16), value_heads, pre...  32.9 us
  transfers between devices with their start and end apart: 7, of which 6 were waited for; matrix products, arithmetic and copies ran while one was open for 5% of the time, Pallas kernels for 0%

commit v1 on v0

v1 whole, which is shorter than its diff:
```python
import functools

import jax
import jax.numpy as jnp
from jax import lax
from jax.experimental import pallas as pl
from jax.experimental.pallas import tpu as pltpu
from jax.sharding import PartitionSpec as P

HD = 128
NEG = -1e30
LOG2E = 1.4426950408889634
SCALE = HD**-0.5 * LOG2E


def attention_kernel(query, query_bias, key, key_hot, value, out):
    left = jnp.concatenate([query[...], query_bias[...]], axis=1)
    right = jnp.concatenate([key[...], key_hot[...]], axis=1)
    scores = lax.dot_general(
        left, right, (((1,), (1,)), ((), ())), preferred_element_type=jnp.float32
    )
    top = jnp.max(scores, axis=1, keepdims=True) * SCALE
    weights = jnp.exp2(scores * SCALE - top)
    total = jnp.sum(weights, axis=1, keepdims=True)
    mixed = jnp.dot(weights.astype(jnp.bfloat16), value[...], preferred_element_type=jnp.float32)
    out[...] = (mixed / total).astype(jnp.bfloat16)


def attention(queries, query_bias, gathered):
    rows, width = queries.shape
    heads = width // HD
    key_rows = gathered.shape[0]
    return pl.pallas_call(
        attention_kernel,
        grid=(heads,),
        out_shape=jax.ShapeDtypeStruct((rows, width), jnp.bfloat16),
        in_specs=[
            pl.BlockSpec((rows, HD), lambda h: (0, h)),
            pl.BlockSpec((rows, HD), lambda h: (0, 0)),
            pl.BlockSpec((key_rows, HD), lambda h: (0, h)),
            pl.BlockSpec((key_rows, HD), lambda h: (0, 2 * heads)),
            pl.BlockSpec((key_rows, HD), lambda h: (0, heads + h)),
        ],
        out_specs=pl.BlockSpec((rows, HD), lambda h: (0, h)),
        compiler_params=pltpu.CompilerParams(vmem_limit_bytes=50 * 1024 * 1024),
    )(queries, query_bias, gathered, gathered, gathered)


def hot_and_bias(cluster_of, pair_mask):
    clusters = pair_mask.shape[0]
    columns = jnp.arange(HD, dtype=jnp.int32)
    hot = cluster_of[:, None] == columns[None, :]
    mask_rows = jnp.dot(
        hot[:, :clusters].astype(jnp.bfloat16),
        (pair_mask != 0).astype(jnp.bfloat16),
        preferred_element_type=jnp.float32,
    )
    bias = jnp.where(mask_rows > 0.5, 0.0, NEG).astype(jnp.bfloat16)
    bias = jnp.pad(bias, ((0, 0), (0, HD - clusters)))
    return hot.astype(jnp.bfloat16), bias


def body(queries, keys, values, cluster_of, pair_mask, out_weight):
    hot, bias = hot_and_bias(cluster_of, pair_mask)
    together = jnp.concatenate([keys, values, hot], axis=1)
    gathered = lax.all_gather(together, "seq", axis=0, tiled=True)
    attn_tok = attention(queries, bias, gathered)
    terms = jnp.dot(attn_tok, out_weight, preferred_element_type=jnp.float32)
    return lax.psum_scatter(terms.astype(jnp.bfloat16), "grp", scatter_dimension=1, tiled=True)


def solution(mesh):
    in_specs = (P("seq", "grp"), P("seq", "grp"), P("seq", "grp"), P("seq"), P(), P("grp", None))
    out_specs = P("seq", "grp")
    return jax.shard_map(body, mesh=mesh, in_specs=in_specs, out_specs=out_specs, check_vma=False)
```

time: 773 us -> 233 us (0.30)
  local copies, waits for them, and re-layouts: 201 us -> 0.03 us
  blocking collectives: 162 us -> 0 us
  matrix products: 87.8 us -> 9.73 us
  waiting for transfers between devices: 254 us -> 192 us
  other arithmetic: 33 us -> 3.29 us
  starting transfers between devices: 15 us -> 0.04 us
  Pallas kernels: 0 us -> 13.4 us
    all_gather x1 -> x0, blocking collectives: 82.5 us -> none  [body(): filled_piece = lax.all_gather(filled, 'seq', axis=0, tiled=True)]
    dot_general x97 -> x1, matrix products: 78.2 us -> 0.15 us  [hot_and_bias(): jnp.dot(hot[:, :clusters].astype(jnp.bfloat16), (pair_mask != 0).astype(j...]
    dynamic_slice x32 -> x0, local copies, waits for them, and re-layouts: 71.3 us -> none  [one_block(): value_block = lax.dynamic_slice_in_dim(value_piece, first_row, span_rows, 0)]
    all_to_all x1 -> x0, blocking collectives: 66 us -> none  [body(): lax.all_to_all(pack_rows(values), 'seq', split_axis=0, concat_axis=0, til...]
    while x224 -> x0, local copies, waits for them, and re-layouts: 61.1 us -> none
    all_to_all x4 -> x0, waiting for transfers between devices: 60 us -> none  [the longest x1 30.5 us: body(): lax.all_to_all(picked, 'seq', split_axis=0, concat_axis=0, tiled=True)]
    unnamed x12 -> x4, local copies, waits for them, and re-layouts: 31.6 us -> 0.01 us
    scatter x8 -> x0, local copies, waits for them, and re-layouts: 24.7 us -> none  [the longest x3 11.2 us: unpack_rows(): return jnp.zeros((panel_size, rows_in.shape[1]), rows_in.dtype).at[got_me...]
  transfers between devices with their start and end apart: 7 -> 2, of which waited for: 6 -> 2; matrix products, arithmetic and copies ran while one was open for 5% -> 0% of each run, Pallas kernels for 0% -> 0%
where the time goes in v1:
time: 233 us; the launch traced here: 232 us
  waiting for transfers between devices  192 us (82%)
  Pallas kernels  13.4 us (6%)
  between operations  13.4 us (6%)
  matrix products  9.73 us (4%)
  other arithmetic  3.29 us (1%)
    all_gather x1, waiting for transfers between devices, body(): gathered = lax.all_gather(together, 'seq', axis=0, tiled=True)  160 us
    reduce_scatter x1, waiting for transfers between devices, body(): lax.psum_scatter(terms.astype(jnp.bfloat16), 'grp', scatter_dimension=1,...  32.7 us
    pallas_call x1, Pallas kernels, attention(): pl.pallas_call(attention_kernel, grid=(heads,), out_shape=jax.ShapeDtypeS...  13.4 us
    dot_general x1, matrix products, body(): terms = jnp.dot(attn_tok, out_weight, preferred_element_type=jnp.float32)  9.58 us
  transfers between devices with their start and end apart: 2, of which 2 were waited for; matrix products, arithmetic and copies ran while one was open for 0% of the time, Pallas kernels for 0%

profile of v1, /device:TPU:0, one launch (start us, length us, event | category | flops | bytes accessed | tf_op | source)
XLA Modules:
  0.0 232.3 jit_solution(11059334152457385660)
XLA Ops:
  6.5 0.0 copy-start.1
  6.5 0.0 copy-start
  6.5 0.0 all-gather.2.cloned.1.call-start
  6.5 0.8 fusion.5
  7.4 2.4 %pad_maximum_fusion = bf16[256,2688]{1,0:T(8,128)(2,1)} fusion(bf16[256,128]{1,0:T(8,128)(2,1)S(1)} %get-tuple-element.5, bf16[256,1280]{1,0:T(8,128)(2,1)} %param.8, bf16[256,1280]{1,0:T(8,128)(2,1)} %param.7), kind=kLoop, calls=%fused_computation.1 | loop fusion | flops 4128768 | bytes 2752512 | tf_op jit(solution)/shard_map/concatenate | solution.py:65
  9.8 0.0 all-gather.2.cloned.1.call-update
  9.9 0.0 reduce-scatter.2.cloned.1.call-start
  9.9 0.0 copy-done.1
  9.9 0.2 fusion.1
  10.1 159.6 %all-gather.2.cloned.1.call-done.key.key_hot.value = bf16[2048,2688]{1,0:T(8,128)(2,1)} async-done(((bf16[256,2688]{1,0:T(8,128)(2,1)}), bf16[2048,2688]{1,0:T(8,128)(2,1)}) %all-gather.2.cloned.1.call-update) | async-done | bytes 11010064 | tf_op jit(solution)/shard_map/all_gather | solution.py:66
  169.7 0.0 copy-done
  169.7 13.4 %shard_map.64 = bf16[256,1280]{1,0:T(8,128)(2,1)S(1)} custom-call(bf16[256,1280]{1,0:T(8,128)(2,1)S(1)} %copy-done, bf16[256,128]{1,0:T(8,128)(2,1)S(1)} %pad.4.query_bias, bf16[2048,2688]{1,0:T(8,128)(2,1)} %all-gather.2.cloned.1.call-done.key.key_hot.value, bf16[2048,2688]{1,0:T(8,128)(2,1)} %all-gather.2.cloned.1.call-done.key.key_hot.value, ...), custom_call_target="tpu_custom_call" | custom-call | tf_op jit(solution)/shard_map/pallas_call | solution.py:33
  183.1 9.6 %convolution_convert_fusion = bf16[256,5120]{1,0:T(8,128)(2,1)} fusion(bf16[256,1280]{1,0:T(8,128)(2,1)S(1)} %shard_map.64, bf16[1280,5120]{1,0:T(8,128)(2,1)} %param.11), kind=kOutput, calls=%fused_computation | convolution fusion | flops 3356753920 | bytes 16384000 | tf_op jit(solution)/shard_map/dot_general | solution.py:68
  192.7 0.0 reduce-scatter.2.cloned.1.call-update
  192.7 32.7 %reduce-scatter.2.cloned.1.call-done = bf16[256,1280]{1,0:T(8,128)(2,1)} async-done(((bf16[256,5120]{1,0:T(8,128)(2,1)}), bf16[256,1280]{1,0:T(8,128)(2,1)}) %reduce-scatter.2.cloned.1.call-update) | async-done | bytes 655376 | tf_op jit(solution)/shard_map/reduce_scatter | solution.py:69
  (1 shorter events, 0.0 us)
Async XLA Ops:
  6.5 3.4 %copy-start.1 = (s32[16,16]{1,0:T(8,128)S(1)}, s32[16,16]{1,0:T(8,128)}, u32[]{:S(2)}) copy-start(s32[16,16]{1,0:T(8,128)} %param.10) | copy-start | bytes 3076
  6.5 163.1 %copy-start = (bf16[256,1280]{1,0:T(8,128)(2,1)S(1)}, bf16[256,1280]{1,0:T(8,128)(2,1)}, u32[]{:S(2)}) copy-start(bf16[256,1280]{1,0:T(8,128)(2,1)} %query.1) | copy-start | bytes 1966084
  6.5 163.1 %all-gather.2.cloned.1.call-start = ((), (), s32[]{:S(2)}) async-start(), calls=%async_computation.1 | async-start | bytes 12386304 | tf_op jit(solution)/shard_map/all_gather | solution.py:66
  9.9 215.6 %reduce-scatter.2.cloned.1.call-start = ((), (), s32[]{:S(2)}) async-start(), calls=%async_computation.2 | async-start | bytes 3276800 | tf_op jit(solution)/shard_map/reduce_scatter | solution.py:69
Sparse Core Ops, SparseCore 0:
  10.0 159.6 all-gather.1
  192.8 32.5 reduce-scatter.1
